TPU v7x, 32 devices: a whole 2x2x4 slice. The times are simulated.
32 devices in a mesh: offset: 8 (over z, x), seg: 4 (over y, core).
Axes of the slice: x: 2, y: 2, z: 4, core: 2. Of those that a mesh axis runs over, the one named last changes fastest.
Arguments:
- traces: bfloat16 [1024, 32, 4096], P('offset', 'seg'), may hold values from -1000 to 1000, as said below
- partners: int32 [8, 3], P('offset'), may hold values from 0 to 7, as said below
Outputs:
- correlations: bfloat16 [24, 128, 128, 129], P('offset', 'seg')
Inputs may be any that keep to these rules, and one draw needn't show every extreme that they name: `traces`: samples of order one to some hundreds; channels and segments differ in level. `partners`: row a holds 3 distinct blocks, each at most 3 blocks from a (a itself may occur); its first entry lies exactly 3 blocks away.
All inputs are finite; a program needn't handle non-finite values.
Results may differ from a plain program's by a relative error of at most 0.0054.
Values may be sent and summed in bfloat16 or wider, within the bound.
A program may use at most 64 MiB of HBM per device.

v0:
```python
import math

import jax
import jax.numpy as jnp
from jax import lax
from jax.sharding import PartitionSpec as P

BINS = 64
SEG_LEN = 4096
FIRST_BIN = 17
HALF_LAG = 64
REACH = 3
PAIR_DEV = 3


def passed_along(array, axis, by):
    devices = lax.axis_size(axis)
    pairs = [(i, i + by) for i in range(devices) if 0 <= i + by < devices]
    return lax.ppermute(array, axis, pairs)


def make_tables(seg_count):
    samples = jnp.arange(SEG_LEN, dtype=jnp.int32)
    bin_index = FIRST_BIN + jnp.arange(BINS, dtype=jnp.int32)
    taper = 0.5 - 0.5 * jnp.cos(2.0 * math.pi * samples.astype(jnp.float32) / SEG_LEN)
    phase = (samples[:, None] * bin_index[None, :] % SEG_LEN).astype(jnp.float32) * (
        2.0 * math.pi / SEG_LEN
    )
    forward = jnp.stack(
        [taper[:, None] * jnp.cos(phase), -taper[:, None] * jnp.sin(phase)], axis=-1
    )
    forward = forward.reshape(SEG_LEN, 2 * BINS).astype(jnp.bfloat16)
    lag_index = jnp.arange(2 * HALF_LAG + 1, dtype=jnp.int32) - HALF_LAG
    turn = (bin_index[:, None] * lag_index[None, :] % SEG_LEN).astype(jnp.float32) * (
        2.0 * math.pi / SEG_LEN
    )
    norm_scale = 1.0 / jnp.sqrt(jnp.float32(seg_count * BINS))
    inverse = jnp.stack([jnp.cos(turn), -jnp.sin(turn)], axis=1) * norm_scale
    inverse = inverse.reshape(2 * BINS, 2 * HALF_LAG + 1).astype(jnp.bfloat16)
    return (forward, inverse)


def cross_spectra(first, second):
    real_part = jnp.einsum(
        "ksi,ksj->kij", first[:, 0], second[:, 0], preferred_element_type=jnp.float32
    )
    real_part = real_part + jnp.einsum(
        "ksi,ksj->kij", first[:, 1], second[:, 1], preferred_element_type=jnp.float32
    )
    imag_part = jnp.einsum(
        "ksi,ksj->kij", first[:, 1], second[:, 0], preferred_element_type=jnp.float32
    )
    imag_part = imag_part - jnp.einsum(
        "ksi,ksj->kij", first[:, 0], second[:, 1], preferred_element_type=jnp.float32
    )
    both = jnp.stack([real_part, imag_part], axis=1)
    return both.reshape(2 * first.shape[0], first.shape[3], second.shape[3]).astype(jnp.bfloat16)


def per_device(traces, partners):
    channels, seg_local, seg_len = traces.shape
    seg_groups = lax.axis_size("seg")
    seg_total = seg_local * seg_groups
    forward, inverse = make_tables(seg_total)
    spectra = jnp.einsum("le,csl->esc", forward, traces, preferred_element_type=jnp.float32)
    spectra = spectra.reshape(BINS, 2, seg_local, channels)
    partial_power = jnp.sum(spectra * spectra, axis=(1, 2))
    bin_power = lax.psum(partial_power, "seg") / seg_total
    whitened = (spectra * lax.rsqrt(bin_power + 1e-06)[:, None, None, :]).astype(jnp.bfloat16)
    whitened = whitened.reshape(2 * BINS, seg_local, channels)
    local_bins = lax.all_to_all(whitened, "seg", split_axis=0, concat_axis=1, tiled=True)
    bins_here = local_bins.shape[0] // 2
    own_block = lax.axis_index("offset")
    received = []
    for distance in range(-REACH, REACH + 1):
        if distance == 0:
            received.append(local_bins)
        else:
            received.append(passed_along(local_bins, "offset", -distance))
    stacked = jnp.stack(received)
    first_slot = REACH - own_block
    own_split = local_bins.reshape(bins_here, 2, seg_total, channels)
    pair_cross = []
    for slot in range(PAIR_DEV):
        position = partners[0, slot] + first_slot
        other = lax.dynamic_index_in_dim(stacked, position, 0, keepdims=False)
        other = other.reshape(bins_here, 2, seg_total, channels)
        pair_cross.append(cross_spectra(own_split, other))
    pair_cross = jnp.stack(pair_cross, axis=1)
    row_split = lax.all_to_all(pair_cross, "seg", split_axis=2, concat_axis=0, tiled=True)
    result = jnp.einsum("epij,el->pijl", row_split, inverse, preferred_element_type=jnp.float32)
    return result.astype(jnp.bfloat16)


def solution(mesh):
    in_specs = (P("offset", "seg", None), P("offset", None))
    out_specs = P("offset", "seg", None, None)
    return jax.shard_map(
        per_device, mesh=mesh, in_specs=in_specs, out_specs=out_specs, check_vma=False
    )
```

profile of v0, /device:TPU:3, one launch (start us, length us, event | category | flops | bytes accessed | tf_op | source)
XLA Modules:
  0.0 130.2 jit_solution(10140744812162280978)
XLA Ops:
  0.1 4.4 %multiply_convert_fusion.1 = (bf16[4096,64,1]{0,1,2:T(8,128)(2,1)S(1)}, bf16[4096,64,1]{0,1,2:T(8,128)(2,1)S(1)}) fusion(s32[64]{0:T(128)S(1)} %iota_add_fusion.1, f32[4096]{0:T(1024)S(1)} %get-tuple-element.19, f32[4096]{0:T(1024)S(1)} %get-tuple-element.20), kind=kLoop, calls=%fused_computation.33 | loop fusion | flops 4718592 | bytes 1081600 | tf_op jit(solution)/shard_map/convert.12
  4.5 1.1 copy.127
  5.6 0.6 reshape.365
  6.3 12.7 %multiply_reduce_fusion = (f32[128,128]{1,0:T(8,128)S(1)}, f32[128,128,8]{1,0,2:T(8,128)S(1)}) fusion(bf16[4096,128,1]{0,1,2:T(8,128)(2,1)S(1)} %reshape.365, bf16[128,8,4096]{2,1,0:T(8,128)(2,1)} %param.2), kind=kOutput, calls=%fused_computation.38 | convolution fusion | flops 1073987584 | bytes 10027008 | tf_op jit(solution)/shard_map/le,csl->esc/dot_general | solution.py:65
  19.1 10.5 %psum.7 = f32[64,128]{1,0:T(8,128)S(1)} all-reduce(f32[64,128]{1,0:T(8,128)S(1)} %reduce_sum.18), channel_id=1, replica_groups=mesh['offset'=8,'seg'=4] {'seg'}, use_global_device_ids=true, to_apply=%region_2.3 | all-reduce | flops 8192 | bytes 65536 | tf_op jit(solution)/shard_map/psum | solution.py:68
  29.8 9.0 %all_to_all.36 = bf16[128,8,128]{2,1,0:T(8,128)(2,1)S(1)} all-to-all(bf16[128,8,128]{2,1,0:T(8,128)(2,1)S(1)} %copy.130), channel_id=1, replica_groups=mesh['offset'=8,'seg'=4] {'seg'}, dimensions={0} | all-to-all | bytes 524288 | tf_op jit(solution)/shard_map/all_to_all | solution.py:71
  38.9 4.2 %collective-permute-start = (bf16[32,32,128]{2,1,0:T(8,128)(2,1)S(1)}, bf16[32,32,128]{2,1,0:T(8,128)(2,1)S(1)}, u32[]{:S(2)}, u32[]{:S(2)}) collective-permute-start(bf16[32,32,128]{2,1,0:T(8,128)(2,1)S(1)} %bitcast.112), channel_id=1, source_target_pairs={{0,12},{4,16},{8,20},{12,24},{16,28},{1,13},{5,17},{9,21},{13,25},... | collective-permute-start | bytes 786440 | tf_op jit(solution)/shard_map/ppermute | solution.py:19
  43.1 3.2 %collective-permute-start.1 = (bf16[32,32,128]{2,1,0:T(8,128)(2,1)S(1)}, bf16[32,32,128]{2,1,0:T(8,128)(2,1)S(1)}, u32[]{:S(2)}, u32[]{:S(2)}) collective-permute-start(bf16[32,32,128]{2,1,0:T(8,128)(2,1)S(1)} %bitcast.113), channel_id=1, source_target_pairs={{0,8},{4,12},{8,16},{12,20},{16,24},{20,28},{1,9},{5,13},{9,17},{1... | collective-permute-start | bytes 786440 | tf_op jit(solution)/shard_map/ppermute | solution.py:19
  46.3 0.7 fusion.35
  48.9 1.3 collective-permute-start.4
  50.2 2.1 %collective-permute-start.3 = (bf16[32,32,128]{2,1,0:T(8,128)(2,1)S(1)}, bf16[32,32,128]{2,1,0:T(8,128)(2,1)S(1)}, u32[]{:S(2)}, u32[]{:S(2)}) collective-permute-start(bf16[32,32,128]{2,1,0:T(8,128)(2,1)S(1)} %bitcast.115), channel_id=1, source_target_pairs={{4,0},{8,4},{12,8},{16,12},{20,16},{24,20},{28,24},{5,1},{9,5},{13... | collective-permute-start | bytes 786440 | tf_op jit(solution)/shard_map/ppermute | solution.py:19
  52.3 4.1 %collective-permute-start.2 = (bf16[32,32,128]{2,1,0:T(8,128)(2,1)S(1)}, bf16[32,32,128]{2,1,0:T(8,128)(2,1)S(1)}, u32[]{:S(2)}, u32[]{:S(2)}) collective-permute-start(bf16[32,32,128]{2,1,0:T(8,128)(2,1)S(1)} %bitcast.116), channel_id=1, source_target_pairs={{0,4},{4,8},{8,12},{12,16},{16,20},{20,24},{24,28},{1,5},{5,9},{9,... | collective-permute-start | bytes 786440 | tf_op jit(solution)/shard_map/ppermute | solution.py:19
  56.4 1.5 %collective-permute-start.5 = (bf16[32,32,128]{2,1,0:T(8,128)(2,1)S(1)}, bf16[32,32,128]{2,1,0:T(8,128)(2,1)S(1)}, u32[]{:S(2)}, u32[]{:S(2)}) collective-permute-start(bf16[32,32,128]{2,1,0:T(8,128)(2,1)S(1)} %bitcast.117), channel_id=1, source_target_pairs={{12,0},{16,4},{20,8},{24,12},{28,16},{13,1},{17,5},{21,9},{25,13},... | collective-permute-start | bytes 786440 | tf_op jit(solution)/shard_map/ppermute | solution.py:19
  58.0 9.9 %collective-permute-done.2 = bf16[32,32,128]{2,1,0:T(8,128)(2,1)S(1)} collective-permute-done((bf16[32,32,128]{2,1,0:T(8,128)(2,1)S(1)}, bf16[32,32,128]{2,1,0:T(8,128)(2,1)S(1)}, u32[]{:S(2)}, u32[]{:S(2)}) %collective-permute-start.2) | collective-permute-done | bytes 262176 | tf_op jit(solution)/shard_map/ppermute | solution.py:19
  68.1 6.7 %collective-permute-done.5 = bf16[32,32,128]{2,1,0:T(8,128)(2,1)S(1)} collective-permute-done((bf16[32,32,128]{2,1,0:T(8,128)(2,1)S(1)}, bf16[32,32,128]{2,1,0:T(8,128)(2,1)S(1)}, u32[]{:S(2)}, u32[]{:S(2)}) %collective-permute-start.5) | collective-permute-done | bytes 262176 | tf_op jit(solution)/shard_map/ppermute | solution.py:19
  77.2 0.4 fusion.8
  77.5 0.4 fusion.9
  78.1 0.4 fusion.12
  80.2 3.7 %copy.145 = bf16[32,3,128,128]{3,0,1,2:T(8,128)(2,1)} copy(bf16[32,3,128,128]{3,2,0,1:T(8,128)(2,1)S(1)} %pad_maximum_fusion) | data formatting | bytes 6291456 | tf_op jit(solution)/shard_map/stack | solution.py:89
  83.9 6.1 %all-to-all-start.1 = ((bf16[32,3,128,128]{3,0,1,2:T(8,128)(2,1)}), bf16[32,3,128,128]{3,0,1,2:T(8,128)(2,1)S(1)}, u32[]{:S(2)}, u32[]{:S(2)}) async-start(bf16[32,3,128,128]{3,0,1,2:T(8,128)(2,1)} %copy.145), calls=%async_computation.1 | async-start | bytes 6291456 | tf_op jit(solution)/shard_map/all_to_all | solution.py:90
  90.6 35.4 %all-to-all-done.1 = bf16[32,3,128,128]{3,0,1,2:T(8,128)(2,1)S(1)} async-done(((bf16[32,3,128,128]{3,0,1,2:T(8,128)(2,1)}), bf16[32,3,128,128]{3,0,1,2:T(8,128)(2,1)S(1)}, u32[]{:S(2)}, u32[]{:S(2)}) %all-to-all-start.1) | async-done | bytes 3145760 | tf_op jit(solution)/shard_map/all_to_all | solution.py:90
  126.0 1.0 copy.147
  127.0 1.1 convolution_convert_fusion
  128.1 2.2 %copy.150 = bf16[3,32,128,129]{2,1,3,0:T(8,128)(2,1)} copy(bf16[3,32,128,129]{2,3,1,0:T(8,128)(2,1)S(1)} %convolution_convert_fusion) | data formatting | bytes 6340608 | tf_op jit(solution)/shard_map/convert_element_type | solution.py:92
  (44 shorter events, 5.4 us)
Async XLA Ops:
  19.0 27.3 %copy-start = (s32[1,3]{1,0:T(1,128)S(1)}, s32[1,3]{1,0:T(1,128)}, u32[]{:S(2)}) copy-start(s32[1,3]{1,0:T(1,128)} %param.3) | copy-start | bytes 40
  38.9 17.5 %collective-permute-start = (bf16[32,32,128]{2,1,0:T(8,128)(2,1)S(1)}, bf16[32,32,128]{2,1,0:T(8,128)(2,1)S(1)}, u32[]{:S(2)}, u32[]{:S(2)}) collective-permute-start(bf16[32,32,128]{2,1,0:T(8,128)(2,1)S(1)} %bitcast.112), channel_id=1, source_target_pairs={{0,12},{4,16},{8,20},{12,24},{16,28},{1,13},{5,17},{9,21},{13,25},... | collective-permute-start | bytes 786440 | tf_op jit(solution)/shard_map/ppermute | solution.py:19
  43.1 14.8 %collective-permute-start.1 = (bf16[32,32,128]{2,1,0:T(8,128)(2,1)S(1)}, bf16[32,32,128]{2,1,0:T(8,128)(2,1)S(1)}, u32[]{:S(2)}, u32[]{:S(2)}) collective-permute-start(bf16[32,32,128]{2,1,0:T(8,128)(2,1)S(1)} %bitcast.113), channel_id=1, source_target_pairs={{0,8},{4,12},{8,16},{12,20},{16,24},{20,28},{1,9},{5,13},{9,17},{1... | collective-permute-start | bytes 786440 | tf_op jit(solution)/shard_map/ppermute | solution.py:19
  48.9 19.2 %collective-permute-start.4 = (bf16[32,32,128]{2,1,0:T(8,128)(2,1)S(1)}, bf16[32,32,128]{2,1,0:T(8,128)(2,1)S(1)}, u32[]{:S(2)}, u32[]{:S(2)}) collective-permute-start(bf16[32,32,128]{2,1,0:T(8,128)(2,1)S(1)} %bitcast.114), channel_id=1, source_target_pairs={{8,0},{12,4},{16,8},{20,12},{24,16},{28,20},{9,1},{13,5},{17,9},{2... | collective-permute-start | bytes 786440 | tf_op jit(solution)/shard_map/ppermute | solution.py:19
  50.2 17.8 %collective-permute-start.3 = (bf16[32,32,128]{2,1,0:T(8,128)(2,1)S(1)}, bf16[32,32,128]{2,1,0:T(8,128)(2,1)S(1)}, u32[]{:S(2)}, u32[]{:S(2)}) collective-permute-start(bf16[32,32,128]{2,1,0:T(8,128)(2,1)S(1)} %bitcast.115), channel_id=1, source_target_pairs={{4,0},{8,4},{12,8},{16,12},{20,16},{24,20},{28,24},{5,1},{9,5},{13... | collective-permute-start | bytes 786440 | tf_op jit(solution)/shard_map/ppermute | solution.py:19
  52.3 15.6 %collective-permute-start.2 = (bf16[32,32,128]{2,1,0:T(8,128)(2,1)S(1)}, bf16[32,32,128]{2,1,0:T(8,128)(2,1)S(1)}, u32[]{:S(2)}, u32[]{:S(2)}) collective-permute-start(bf16[32,32,128]{2,1,0:T(8,128)(2,1)S(1)} %bitcast.116), channel_id=1, source_target_pairs={{0,4},{4,8},{8,12},{12,16},{16,20},{20,24},{24,28},{1,5},{5,9},{9,... | collective-permute-start | bytes 786440 | tf_op jit(solution)/shard_map/ppermute | solution.py:19
  56.4 18.5 %collective-permute-start.5 = (bf16[32,32,128]{2,1,0:T(8,128)(2,1)S(1)}, bf16[32,32,128]{2,1,0:T(8,128)(2,1)S(1)}, u32[]{:S(2)}, u32[]{:S(2)}) collective-permute-start(bf16[32,32,128]{2,1,0:T(8,128)(2,1)S(1)} %bitcast.117), channel_id=1, source_target_pairs={{12,0},{16,4},{20,8},{24,12},{28,16},{13,1},{17,5},{21,9},{25,13},... | collective-permute-start | bytes 786440 | tf_op jit(solution)/shard_map/ppermute | solution.py:19
  83.9 42.1 %all-to-all-start.1 = ((bf16[32,3,128,128]{3,0,1,2:T(8,128)(2,1)}), bf16[32,3,128,128]{3,0,1,2:T(8,128)(2,1)S(1)}, u32[]{:S(2)}, u32[]{:S(2)}) async-start(bf16[32,3,128,128]{3,0,1,2:T(8,128)(2,1)} %copy.145), calls=%async_computation.1 | async-start | bytes 6291456 | tf_op jit(solution)/shard_map/all_to_all | solution.py:90
where the time goes:
time: 131 us; the launch traced here: 130 us
  waiting for transfers between devices  52.1 us (40%)
  starting transfers between devices  22.5 us (17%)
  blocking collectives  19.5 us (15%)
  matrix products  18 us (14%)
  local copies, waits for them, and re-layouts  10.2 us (8%)
  other arithmetic  5.66 us (4%)
  between operations  2.32 us (2%)
    all_to_all x1, waiting for transfers between devices, per_device(): lax.all_to_all(pair_cross, 'seg', split_axis=2, concat_axis=0, tiled=True)  35.4 us
    ppermute x6, waiting for transfers between devices, passed_along(): return lax.ppermute(array, axis, pairs)  16.7 us
    ppermute x6, starting transfers between devices, passed_along(): return lax.ppermute(array, axis, pairs)  16.4 us
    dot_general x1, matrix products, per_device(): jnp.einsum('le,csl->esc', forward, traces, preferred_element_type=jnp.flo...  12.7 us
    psum x1, blocking collectives, per_device(): bin_power = lax.psum(partial_power, 'seg') / seg_total  10.5 us
    all_to_all x1, blocking collectives, per_device(): lax.all_to_all(whitened, 'seg', split_axis=0, concat_axis=1, tiled=True)  9.02 us
    all_to_all x1, starting transfers between devices, per_device(): lax.all_to_all(pair_cross, 'seg', split_axis=2, concat_axis=0, tiled=True)  6.12 us
    another operation x1, other arithmetic  4.35 us
  transfers between devices with their start and end apart: 7, of which 3 were waited for; matrix products, arithmetic and copies ran while one was open for 1% of the time, Pallas kernels for 0%

commit v1 on v0

v1 whole, which is shorter than its diff:
```python
import functools
import math

import jax
import jax.numpy as jnp
import numpy as np
from jax import lax
from jax.experimental import pallas as pl
from jax.experimental.pallas import tpu as pltpu
from jax.sharding import PartitionSpec as P

BINS = 64
FIRST_BIN = 17
HALF_LAG = 64
REACH = 3
PAIR_DEV = 3
CORES = 2
MESH = pl.DeviceIdType.MESH


def make_tables(seg_count, seg_len):
    samples = np.arange(seg_len, dtype=np.int64)
    bin_index = FIRST_BIN + np.arange(BINS, dtype=np.int64)
    taper = 0.5 - 0.5 * np.cos(2.0 * math.pi * samples / seg_len)
    phase = (samples[:, None] * bin_index[None, :] % seg_len) * (2.0 * math.pi / seg_len)
    forward = np.concatenate(
        [taper[:, None] * np.cos(phase), -taper[:, None] * np.sin(phase)], axis=1
    )
    lag_index = np.arange(2 * HALF_LAG + 1, dtype=np.int64) - HALF_LAG
    turn = (bin_index[:, None] * lag_index[None, :] % seg_len) * (2.0 * math.pi / seg_len)
    scale = 1.0 / math.sqrt(seg_count * BINS)
    inverse = np.concatenate([np.cos(turn), -np.sin(turn)], axis=0) * scale
    return forward.astype(np.float32).astype(jnp.bfloat16), inverse.astype(np.float32).astype(jnp.bfloat16)


def spectra_kernel(seg_local, traces_ref, table_ref, out_ref, flat, turned):
    step = pl.program_id(0)
    rows = traces_ref.shape[0]
    entries = table_ref.shape[1]
    flat[pl.ds(pl.multiple_of(step * rows, rows), rows), :] = jnp.dot(
        traces_ref[...], table_ref[...], preferred_element_type=jnp.float32
    )

    @pl.when(step == pl.num_programs(0) - 1)
    def _():
        channels = flat.shape[0] // seg_local
        for seg in range(seg_local):
            one = flat[pl.ds(seg, channels, stride=seg_local), :]
            turned[pl.ds(seg, entries, stride=seg_local), :] = one.T
        out_ref[...] = turned[...].astype(out_ref.dtype)


def spectra_of(traces, forward):
    channels, seg_local, seg_len = traces.shape
    rows = channels * seg_local
    entries = forward.shape[1]
    tile = 128
    return pl.pallas_call(
        functools.partial(spectra_kernel, seg_local),
        grid=(rows // tile,),
        in_specs=[
            pl.BlockSpec((tile, seg_len), lambda i: (i, 0)),
            pl.BlockSpec((seg_len, entries), lambda i: (0, 0)),
        ],
        out_specs=pl.BlockSpec((entries * seg_local, channels), lambda i: (0, 0)),
        out_shape=jax.ShapeDtypeStruct((entries * seg_local, channels), jnp.bfloat16),
        scratch_shapes=[
            pltpu.VMEM((rows, entries), jnp.float32),
            pltpu.VMEM((entries * seg_local, channels), jnp.float32),
        ],
    )(traces.reshape(rows, seg_len), forward)


def gather_kernel(blocks, segs, own_ref, out_ref, send_sem, recv_sem, mate_sem, local_sem):
    groups = segs // CORES
    block = lax.axis_index("offset")
    seg = lax.axis_index("seg")
    group, core = seg // CORES, seg % CORES
    toward = 2 * (block % 2) - 1
    others = list(range(1, groups))

    def exists(u):
        return jnp.logical_and(block + u * toward >= 0, block + u * toward < blocks)

    def seg_of(g, which):
        return (group + g) % groups * CORES + which

    def slot(u, g, which):
        return out_ref.at[REACH + u * toward, seg_of(g, which)]

    sent = []

    def send(u, g, to_block, to_seg, sem, guard):
        number = len(sent)

        def make():
            return pltpu.make_async_remote_copy(
                src_ref=own_ref if (u, g) == (0, 0) else slot(u, g, core),
                dst_ref=out_ref.at[REACH + block + u * toward - to_block, seg_of(g, core)],
                send_sem=send_sem.at[number],
                recv_sem=sem,
                device_id=(to_block, to_seg),
                device_id_type=MESH,
            )

        sent.append((guard, make))
        when(guard, lambda: make().start())

    def when(guard, do):
        if guard is None:
            do()
        else:
            pl.when(guard)(do)

    def both(*guards):
        kept = [guard for guard in guards if guard is not None]
        return functools.reduce(jnp.logical_and, kept) if kept else None

    def here(u):
        return None if u in (0, -1) else exists(u)

    def back(u, g, at):
        send(u, g, block - 2 * toward, seg, recv_sem.at[at + REACH, g], both(exists(-2), here(u)))

    def ahead(u, g, at):
        send(u, g, block + 2 * toward, seg, recv_sem.at[at + REACH, g], both(exists(2), here(u)))

    def beside(u, g, at):
        send(u, g, block - toward, seg, recv_sem.at[at + REACH, g], here(u))

    def across(u):
        for g in others:
            to_seg = (group - g + groups) % groups * CORES + core
            send(u, 0, block, to_seg, recv_sem.at[u + REACH, g], here(u))

    def swap(u, g):
        send(u, g, block, group * CORES + 1 - core, mate_sem.at[u + REACH, g], here(u))

    def arrived(u, g):
        def wait():
            pltpu.make_async_copy(
                slot(u, g, core), slot(u, g, core), recv_sem.at[u + REACH, g]
            ).wait()

        when(here(u), wait)
        swap(u, g)

    barrier = pltpu.get_barrier_semaphore()

    def greet(to_block, to_seg):
        pl.semaphore_signal(barrier, inc=1, device_id=(to_block, to_seg), device_id_type=MESH)

    greet(block, group * CORES + 1 - core)
    greet(block - toward, seg)
    for g in others:
        greet(block, seg_of(g, core))
    for u in (-2, 2):

        @pl.when(exists(u))
        def _():
            greet(block + u * toward, seg)

    ends = exists(-2).astype(jnp.int32) + exists(2).astype(jnp.int32)
    pl.semaphore_wait(barrier, 2 + len(others) + ends)

    back(0, 0, 2)
    ahead(0, 0, -2)
    beside(0, 0, -1)
    across(0)
    swap(0, 0)
    keep = pltpu.make_async_copy(own_ref, slot(0, 0, core), local_sem)
    keep.start()

    arrived(-1, 0)
    back(-1, 0, 1)
    ahead(-1, 0, -3)
    across(-1)
    for g in others:
        arrived(0, g)
        ahead(0, g, -2)
    arrived(2, 0)
    arrived(-2, 0)
    arrived(1, 0)
    back(1, 0, 3)
    for g in others:
        back(0, g, 2)
    for g in others:
        arrived(-1, g)
        ahead(-1, g, -3)
    arrived(-3, 0)
    arrived(3, 0)
    across(3)
    for g in others:
        arrived(-2, g)
        beside(-2, g, 1)
    for u in (2, -3, 1, 3):
        for g in others:
            arrived(u, g)

    keep.wait()
    for u in range(-REACH, REACH + 1):
        for g in range(groups):

            def wait(u=u, g=g):
                pltpu.make_async_copy(
                    slot(u, g, 1 - core), slot(u, g, 1 - core), mate_sem.at[u + REACH, g]
                ).wait()

            when(here(u), wait)
    for guard, make in sent:
        when(guard, lambda make=make: make().wait_send())


def gathered(chunk, blocks, segs):
    groups = segs // CORES
    sends = (5 + 2 * REACH + 1) * groups + 8 * groups + 8
    width = 2 * REACH + 1
    return pl.pallas_call(
        functools.partial(gather_kernel, blocks, segs),
        out_shape=jax.ShapeDtypeStruct((width, segs) + chunk.shape, chunk.dtype),
        in_specs=[pl.BlockSpec(memory_space=pltpu.VMEM)],
        out_specs=pl.BlockSpec(memory_space=pl.ANY),
        scratch_shapes=[
            pltpu.SemaphoreType.DMA((sends,)),
            pltpu.SemaphoreType.DMA((width, groups)),
            pltpu.SemaphoreType.DMA((width, groups)),
            pltpu.SemaphoreType.DMA,
        ],
        compiler_params=pltpu.CompilerParams(collective_id=0, has_side_effects=True),
    )(chunk)


def cross_kernel(seg_total, place_ref, own_ref, *rest):
    other_refs, out_ref = rest[:-1], rest[-1]
    bins = own_ref.shape[1]
    half = own_ref.shape[3] // 2

    for k in range(bins):
        parts = []
        for ref in other_refs:
            block = ref[0, :, :, k].astype(jnp.float32)
            block = block.reshape(-1, block.shape[-1])
            power = jnp.sum(block * block, axis=0, keepdims=True) / seg_total
            parts.append((block * lax.rsqrt(power + 1e-06)).astype(jnp.bfloat16))
        other = jnp.concatenate(parts, axis=1)
        product = lax.dot_general(
            own_ref[0, k], other, (((0,), (0,)), ((), ())), preferred_element_type=jnp.float32
        ).astype(out_ref.dtype)
        channels = parts[0].shape[1]
        for pair in range(len(parts)):
            piece = product[:, pair * channels : (pair + 1) * channels]
            out_ref[0, k, pair] = piece[:half]
            out_ref[1, k, pair] = piece[half:]


def cross_of(places, own, around, rows, seg_total):
    width, segs, _, bins, seg_local, channels = around.shape
    tile = 8

    def other(pair):
        return pl.BlockSpec(
            (1, segs, 2, tile, seg_local, channels),
            lambda i, place, pair=pair: (place[pair], 0, 0, i, 0, 0),
        )

    depth, columns = own.shape[2:]
    return pl.pallas_call(
        functools.partial(cross_kernel, seg_total),
        grid_spec=pltpu.PrefetchScalarGridSpec(
            num_scalar_prefetch=1,
            grid=(bins // tile,),
            in_specs=[pl.BlockSpec((1, tile, depth, columns), lambda i, place: (0, i, 0, 0))]
            + [other(pair) for pair in range(PAIR_DEV)],
            out_specs=pl.BlockSpec(
                (2, tile, PAIR_DEV, rows, channels), lambda i, place: (0, i, 0, 0, 0)
            ),
        ),
        out_shape=jax.ShapeDtypeStruct((2, bins, PAIR_DEV, rows, channels), jnp.bfloat16),
    )(places, own, *([around] * PAIR_DEV))


def per_device(traces, partners):
    channels, seg_local, seg_len = traces.shape
    segs = lax.axis_size("seg")
    blocks = lax.axis_size("offset")
    seg_total = seg_local * segs
    rows = channels // segs
    forward, inverse = make_tables(seg_total, seg_len)
    chunk = spectra_of(traces, jnp.asarray(forward))
    around = gathered(chunk, blocks, segs)
    around = around.reshape(2 * REACH + 1, segs, 2, BINS, seg_local, channels)
    own = lax.dynamic_slice_in_dim(around[REACH], lax.axis_index("seg") * rows, rows, axis=4)
    own = own.astype(jnp.float32)
    power = jnp.sum(own * own, axis=(0, 1, 3)) / seg_total
    own = own * lax.rsqrt(power + 1e-06)[None, None, :, None, :]
    real, imag = own[:, 0], own[:, 1]
    left = jnp.stack([jnp.stack([real, imag], axis=1), jnp.stack([imag, -real], axis=1)], axis=4)
    left = left.transpose(2, 0, 1, 3, 4, 5).reshape(1, BINS, segs * 2 * seg_local, 2 * rows)
    places = partners[0] + REACH - lax.axis_index("offset")
    cross = cross_of(places, left.astype(jnp.bfloat16), around, rows, seg_total)
    cross = cross.reshape(2 * BINS, PAIR_DEV, rows, channels)
    result = jnp.einsum(
        "epij,el->pijl", cross, jnp.asarray(inverse), preferred_element_type=jnp.float32
    )
    return result.astype(jnp.bfloat16)


def solution(mesh):
    in_specs = (P("offset", "seg", None), P("offset", None))
    out_specs = P("offset", "seg", None, None)
    return jax.shard_map(
        per_device, mesh=mesh, in_specs=in_specs, out_specs=out_specs, check_vma=False
    )
```

time: 131 us -> 64.5 us (0.49)
  waiting for transfers between devices: 52.1 us -> 0 us
  Pallas kernels: 0 us -> 51.3 us
  starting transfers between devices: 22.5 us -> 0 us
  blocking collectives: 19.5 us -> 0 us
  matrix products: 18 us -> 3.38 us
  other arithmetic: 5.66 us -> 1.87 us
  local copies, waits for them, and re-layouts: 10.2 us -> 6.88 us
  between operations: 2.32 us -> 0.08 us
    pallas_call x0 -> x3, Pallas kernels: none -> 51.3 us  [the longest x1 34.5 us: gathered(): pl.pallas_call(functools.partial(gather_kernel, blocks, segs), out_shape=...]
    all_to_all x1 -> x0, waiting for transfers between devices: 35.4 us -> none  [per_device(): lax.all_to_all(pair_cross, 'seg', split_axis=2, concat_axis=0, tiled=True)]
    ppermute x6 -> x0, waiting for transfers between devices: 16.7 us -> none  [passed_along(): return lax.ppermute(array, axis, pairs)]
    ppermute x6 -> x0, starting transfers between devices: 16.4 us -> none  [passed_along(): return lax.ppermute(array, axis, pairs)]
    dot_general x14 -> x1, matrix products: 18 us -> 3.38 us  [per_device(): jnp.einsum('epij,el->pijl', cross, jnp.asarray(inverse), preferred_elemen...]
    psum x1 -> x0, blocking collectives: 10.5 us -> none  [per_device(): bin_power = lax.psum(partial_power, 'seg') / seg_total]
    all_to_all x1 -> x0, blocking collectives: 9.02 us -> none  [per_device(): lax.all_to_all(whitened, 'seg', split_axis=0, concat_axis=1, tiled=True)]
    all_to_all x1 -> x0, starting transfers between devices: 6.12 us -> none  [per_device(): lax.all_to_all(pair_cross, 'seg', split_axis=2, concat_axis=0, tiled=True)]
  transfers between devices with their start and end apart: 7 -> 0, of which waited for: 3 -> 0; matrix products, arithmetic and copies ran while one was open for 1% -> 0% of each run, Pallas kernels for 0% -> 0%
where the time goes in v1:
time: 64.5 us; the launch traced here: 63.5 us
  Pallas kernels  51.3 us (80%)
  local copies, waits for them, and re-layouts  6.88 us (11%)
  matrix products  3.38 us (5%)
  other arithmetic  1.87 us (3%)
    pallas_call x1, Pallas kernels, gathered(): pl.pallas_call(functools.partial(gather_kernel, blocks, segs), out_shape=...  34.5 us
    pallas_call x1, Pallas kernels, spectra_of(): pl.pallas_call(functools.partial(spectra_kernel, seg_local), grid=(rows /...  8.55 us
    pallas_call x1, Pallas kernels, cross_of(): pl.pallas_call(functools.partial(cross_kernel, seg_total), grid_spec=pltp...  8.22 us
    dot_general x1, matrix products, per_device(): jnp.einsum('epij,el->pijl', cross, jnp.asarray(inverse), preferred_elemen...  3.38 us
    convert_element_type x1, local copies, waits for them, and re-layouts, per_device(): cross = cross_of(places, left.astype(jnp.bfloat16), around, rows, seg_total)  2.38 us
    convert_element_type x1, local copies, waits for them, and re-layouts, per_device(): return result.astype(jnp.bfloat16)  2.19 us
    slice x1, local copies, waits for them, and re-layouts, per_device(): around[REACH]  1.3 us

profile of v1, /device:TPU:3, one launch (start us, length us, event | category | flops | bytes accessed | tf_op | source)
XLA Modules:
  0.0 63.5 jit_solution(13413138907504075339)
XLA Ops:
  0.0 1.1 %subtract_bitcast_fusion.place_ref = s32[3]{0:T(128)} fusion(s32[1,3]{1,0:T(1,128)} %param.5, s32[]{:T(128)S(6)} %axis_index.23), kind=kLoop, calls=%fused_computation.12 | loop fusion | flops 6 | bytes 28 | tf_op jit(solution)/shard_map/sub | solution.py:299
  1.1 8.5 %shard_map.46.own_ref = bf16[1024,128]{1,0:T(8,128)(2,1)} custom-call(bf16[1024,4096]{1,0:T(8,128)(2,1)} %bitcast.20, bf16[4096,128]{1,0:T(8,128)(2,1)} %constant.28.clone.table_ref), custom_call_target="tpu_custom_call" | custom-call | tf_op jit(solution)/shard_map/pallas_call | solution.py:58
  9.7 34.5 %shard_map.47 = bf16[7,4,1024,128]{3,2,1,0:T(8,128)(2,1)} custom-call(bf16[1024,128]{1,0:T(8,128)(2,1)} %shard_map.46.own_ref), custom_call_target="tpu_custom_call" | custom-call | tf_op jit(solution)/shard_map/pallas_call | solution.py:218
  44.2 1.3 %slice.12 = bf16[1,4,1024,128]{3,2,1,0:T(8,128)(2,1)S(1)} slice(bf16[7,4,1024,128]{3,2,1,0:T(8,128)(2,1)} %shard_map.47), slice={[3:4], [0:4], [0:1024], [0:128]} | slice | bytes 2097152 | tf_op jit(solution)/shard_map/slice | solution.py:292
  45.5 0.4 constant_dynamic-slice_fusion
  45.9 0.6 copy.14
  46.5 0.2 fusion.5
  46.7 0.2 fusion.7
  46.9 0.1 fusion.6
  47.0 0.1 maximum_bitcast_fusion
  47.1 0.2 pad_maximum_fusion
  47.3 2.4 %copy.10.own_ref = bf16[1,64,64,64]{3,2,1,0:T(8,128)(2,1)} copy(bf16[1,64,64,64]{1,3,2,0:T(8,128)(2,1)S(1)} %bitcast.22) | data formatting | bytes 1048576 | tf_op jit(solution)/shard_map/convert_element_type | solution.py:300
  49.7 0.0 copy-start
  49.7 8.2 %shard_map.48 = bf16[2,64,3,32,128]{4,3,2,1,0:T(8,128)(2,1)} custom-call(s32[3]{0:T(128)} %subtract_bitcast_fusion.place_ref, bf16[1,64,64,64]{3,2,1,0:T(8,128)(2,1)} %copy.10.own_ref, bf16[7,4,2,64,8,128]{5,4,3,2,1,0:T(8,128)(2,1)} %bitcast.16, bf16[7,4,2,64,8,128]{5,4,3,2,1,0:T(8,128)(2,1)} %bitcast.17, bf16[7,4,2,64,8,128]{5,4,3,2,1,0:T(8,128)(2,1)} %bitcast.18), custom_call_target="tpu_custom_call" | custom-call | tf_op jit(solution)/shard_map/pallas_call | solution.py:267
  57.9 0.0 copy-done
  57.9 3.4 %fusion.2 = bf16[3,32,128,129]{2,3,1,0:T(8,128)(2,1)S(1)} fusion(bf16[128,129,1,1]{0,1,3,2:T(8,128)(2,1)S(1)} %copy-done, bf16[128,3,32,128]{3,2,1,0:T(8,128)(2,1)} %bitcast.19), kind=kOutput, calls=%fused_computation.2 | convolution fusion | flops 407384064 | bytes 6349056 | tf_op jit(solution)/shard_map/epij,el->pijl/dot_general | solution.py:302
  61.3 2.2 %copy.12 = bf16[3,32,128,129]{2,1,3,0:T(8,128)(2,1)} copy(bf16[3,32,128,129]{2,3,1,0:T(8,128)(2,1)S(1)} %fusion.2) | data formatting | bytes 6340608 | tf_op jit(solution)/shard_map/convert_element_type | solution.py:305
  (2 shorter events, 0.0 us)
Async XLA Ops:
  49.7 8.2 %copy-start = (bf16[128,129,1,1]{0,1,3,2:T(8,128)(2,1)S(1)}, bf16[128,129,1,1]{0,1,3,2:T(8,128)(2,1)}, u32[]{:S(2)}) copy-start(bf16[128,129,1,1]{0,1,3,2:T(8,128)(2,1)} %constant.31) | copy-start | bytes 99076

commit v2 on v1

v2 whole, which is shorter than its diff:
```python
import functools
import math

import jax
import jax.numpy as jnp
import numpy as np
from jax import lax
from jax.experimental import pallas as pl
from jax.experimental.pallas import tpu as pltpu
from jax.sharding import PartitionSpec as P

BINS = 64
FIRST_BIN = 17
HALF_LAG = 64
REACH = 3
PAIR_DEV = 3
CORES = 2
HALVES = 2
MESH = pl.DeviceIdType.MESH


def make_tables(seg_count, seg_len):
    samples = np.arange(seg_len, dtype=np.int64)
    bin_index = FIRST_BIN + np.arange(BINS, dtype=np.int64)
    taper = 0.5 - 0.5 * np.cos(2.0 * math.pi * samples / seg_len)
    phase = (samples[:, None] * bin_index[None, :] % seg_len) * (2.0 * math.pi / seg_len)
    forward = np.concatenate(
        [taper[:, None] * np.cos(phase), -taper[:, None] * np.sin(phase)], axis=1
    )
    lag_index = np.arange(2 * HALF_LAG + 1, dtype=np.int64) - HALF_LAG
    turn = (bin_index[:, None] * lag_index[None, :] % seg_len) * (2.0 * math.pi / seg_len)
    scale = 1.0 / math.sqrt(seg_count * BINS)
    inverse = np.concatenate([np.cos(turn), -np.sin(turn)], axis=0) * scale
    return forward.astype(np.float32).astype(jnp.bfloat16), inverse.astype(np.float32).astype(jnp.bfloat16)


def spectra_kernel(seg_local, traces_ref, table_ref, out_ref, flat, turned):
    step = pl.program_id(0)
    entries = table_ref.shape[1]
    part = jnp.dot(traces_ref[...], table_ref[...], preferred_element_type=jnp.float32)

    @pl.when(step == 0)
    def _():
        flat[...] = part

    @pl.when(step > 0)
    def _():
        flat[...] += part

    @pl.when(step == pl.num_programs(0) - 1)
    def _():
        channels = flat.shape[0] // seg_local
        for seg in range(seg_local):
            one = flat[pl.ds(seg, channels, stride=seg_local), :]
            turned[pl.ds(seg, entries, stride=seg_local), :] = one.T
        out_ref[...] = turned[...].astype(out_ref.dtype)


def spectra_of(traces, forward):
    channels, seg_local, seg_len = traces.shape
    rows = channels * seg_local
    entries = forward.shape[1]
    tile = 512
    return pl.pallas_call(
        functools.partial(spectra_kernel, seg_local),
        grid=(seg_len // tile,),
        in_specs=[
            pl.BlockSpec((rows, tile), lambda i: (0, i)),
            pl.BlockSpec((tile, entries), lambda i: (i, 0)),
        ],
        out_specs=pl.BlockSpec((entries * seg_local, channels), lambda i: (0, 0)),
        out_shape=jax.ShapeDtypeStruct((entries * seg_local, channels), jnp.bfloat16),
        scratch_shapes=[
            pltpu.VMEM((rows, entries), jnp.float32),
            pltpu.VMEM((entries * seg_local, channels), jnp.float32),
        ],
    )(traces.reshape(rows, seg_len), forward)


def gather_kernel(blocks, segs, own_ref, out_ref, send_sem, recv_sem, mate_sem, local_sem):
    groups = segs // CORES
    block = lax.axis_index("offset")
    seg = lax.axis_index("seg")
    group, core = seg // CORES, seg % CORES
    toward = 2 * (block % 2) - 1
    others = list(range(1, groups))

    def exists(u):
        return jnp.logical_and(block + u * toward >= 0, block + u * toward < blocks)

    def seg_of(g, which):
        return (group + g) % groups * CORES + which

    half = own_ref.shape[0] // HALVES

    def part(h):
        return pl.ds(h * half, half)

    def slot(u, g, h, which):
        return out_ref.at[REACH + u * toward, seg_of(g, which), part(h)]

    sent = []

    def when(guard, do):
        if guard is None:
            do()
        else:
            pl.when(guard)(do)

    def both(*guards):
        kept = [guard for guard in guards if guard is not None]
        return functools.reduce(jnp.logical_and, kept) if kept else None

    def here(u):
        return None if u in (0, -1) else exists(u)

    def send(u, g, h, to_block, to_seg, sem, guard):
        number = len(sent)

        def make():
            return pltpu.make_async_remote_copy(
                src_ref=own_ref.at[part(h)] if (u, g) == (0, 0) else slot(u, g, h, core),
                dst_ref=out_ref.at[
                    REACH + block + u * toward - to_block, seg_of(g, core), part(h)
                ],
                send_sem=send_sem.at[number],
                recv_sem=sem,
                device_id=(to_block, to_seg),
                device_id_type=MESH,
            )

        sent.append((guard, make))
        when(guard, lambda: make().start())

    def back(u, g, h):
        at = recv_sem.at[u + 2 + REACH, g, h]
        send(u, g, h, block - 2 * toward, seg, at, both(exists(-2), here(u)))

    def ahead(u, g, h):
        at = recv_sem.at[u - 2 + REACH, g, h]
        send(u, g, h, block + 2 * toward, seg, at, both(exists(2), here(u)))

    def beside(u, g, h):
        at = recv_sem.at[-1 - u + REACH, g, h]
        send(u, g, h, block - toward, seg, at, here(u))

    def across(u, h):
        for g in others:
            to_seg = (group - g + groups) % groups * CORES + core
            send(u, 0, h, block, to_seg, recv_sem.at[u + REACH, g, h], here(u))

    def swap(u, g, h):
        at = mate_sem.at[u + REACH, g, h]
        send(u, g, h, block, group * CORES + 1 - core, at, here(u))

    def arrived(u, g, h):
        def wait():
            here_now = slot(u, g, h, core)
            pltpu.make_async_copy(here_now, here_now, recv_sem.at[u + REACH, g, h]).wait()

        when(here(u), wait)
        swap(u, g, h)

    barrier = pltpu.get_barrier_semaphore()

    def greet(to_block, to_seg):
        pl.semaphore_signal(barrier, inc=1, device_id=(to_block, to_seg), device_id_type=MESH)

    greet(block, group * CORES + 1 - core)
    greet(block - toward, seg)
    for g in others:
        greet(block, seg_of(g, core))
    for u in (-2, 2):

        @pl.when(exists(u))
        def _():
            greet(block + u * toward, seg)

    ends = exists(-2).astype(jnp.int32) + exists(2).astype(jnp.int32)
    pl.semaphore_wait(barrier, 2 + len(others) + ends)

    every = range(HALVES)
    for h in every:
        across(0, h)
        beside(0, 0, h)
        back(0, 0, h)
        ahead(0, 0, h)
    for h in every:
        swap(0, 0, h)
    whole = out_ref.at[REACH, seg]
    keep = pltpu.make_async_copy(own_ref, whole, local_sem)
    keep.start()

    for h in every:
        arrived(-1, 0, h)
        back(-1, 0, h)
        ahead(-1, 0, h)
        for g in others:
            arrived(0, g, h)
            beside(0, g, h)
        arrived(2, 0, h)
        if h >= HALVES // 2:
            across(2, h)
        arrived(-2, 0, h)
    for g in others:
        for h in every:
            ahead(0, g, h)
    for h in every:
        arrived(1, 0, h)
        back(1, 0, h)
        arrived(-3, 0, h)
        if h >= HALVES // 2:
            across(-3, h)
    for g in others:
        for h in range(HALVES // 2):
            back(0, g, h)
    for h in every:
        for g in others:
            arrived(-1, g, h)
            if h < HALVES // 2:
                ahead(-1, g, h)
    for g in others:
        for h in range(HALVES // 2, HALVES):
            arrived(2, g, h)
    for h in every:
        arrived(3, 0, h)
        across(3, h)
        for g in others:
            arrived(-2, g, h)
            beside(-2, g, h)
    for g in others:
        for h in range(HALVES // 2, HALVES):
            arrived(-3, g, h)
        for h in range(HALVES // 2):
            arrived(2, g, h)
            arrived(-3, g, h)
        for h in every:
            arrived(1, g, h)
            arrived(3, g, h)

    keep.wait()
    for u in range(-REACH, REACH + 1):
        for g in range(groups):
            for h in every:

                def wait(u=u, g=g, h=h):
                    theirs = slot(u, g, h, 1 - core)
                    pltpu.make_async_copy(
                        theirs, theirs, mate_sem.at[u + REACH, g, h]
                    ).wait()

                when(here(u), wait)
    for guard, make in sent:
        when(guard, lambda make=make: make().wait_send())


def gathered(chunk, blocks, segs):
    groups = segs // CORES
    sends = (16 * groups + 8) * HALVES
    width = 2 * REACH + 1
    return pl.pallas_call(
        functools.partial(gather_kernel, blocks, segs),
        out_shape=jax.ShapeDtypeStruct((width, segs) + chunk.shape, chunk.dtype),
        in_specs=[pl.BlockSpec(memory_space=pltpu.VMEM)],
        out_specs=pl.BlockSpec(memory_space=pl.ANY),
        scratch_shapes=[
            pltpu.SemaphoreType.DMA((sends,)),
            pltpu.SemaphoreType.DMA((width, groups, HALVES)),
            pltpu.SemaphoreType.DMA((width, groups, HALVES)),
            pltpu.SemaphoreType.DMA,
        ],
        compiler_params=pltpu.CompilerParams(collective_id=0, has_side_effects=True),
    )(chunk)


def whitened(ref, k, seg_total):
    block = ref[0, :, :, k].astype(jnp.float32)
    block = block.reshape(-1, block.shape[-1])
    power = jnp.sum(block * block, axis=0, keepdims=True) / seg_total
    return block * lax.rsqrt(power + 1e-06)


def cross_kernel(seg_total, rows, partners_ref, own_ref, *rest):
    other_refs, out_ref = rest[:-1], rest[-1]
    segs, _, bins, seg_local, channels = own_ref.shape[1:]
    shift = (channels - lax.axis_index("seg") * rows) % channels
    lane = lax.broadcasted_iota(jnp.int32, (segs * 2 * seg_local, channels), 1)

    for k in range(bins):
        own = pltpu.roll(whitened(own_ref, k, seg_total), shift, 1)
        split = own.reshape(segs, 2, seg_local, channels)
        turned = jnp.stack([split[:, 1], -split[:, 0]], axis=1).reshape(own.shape)
        own = jnp.where(lane < rows, own, pltpu.roll(turned, rows, 1))
        own = own[:, : 2 * rows].astype(jnp.bfloat16)
        parts = [whitened(ref, k, seg_total).astype(jnp.bfloat16) for ref in other_refs]
        product = lax.dot_general(
            own,
            jnp.concatenate(parts, axis=1),
            (((0,), (0,)), ((), ())),
            preferred_element_type=jnp.float32,
        ).astype(out_ref.dtype)
        for pair in range(len(parts)):
            piece = product[:, pair * channels : (pair + 1) * channels]
            out_ref[0, k, pair] = piece[:rows]
            out_ref[1, k, pair] = piece[rows:]


def cross_of(partners, around, rows, seg_total):
    width, segs, _, bins, seg_local, channels = around.shape
    tile = 16

    def part_of(place):
        return pl.BlockSpec(
            (1, segs, 2, tile, seg_local, channels),
            lambda i, partners: (place(partners), 0, 0, i, 0, 0),
        )

    def other(pair):
        return part_of(lambda partners: partners[0, pair] + REACH - lax.axis_index("offset"))

    return pl.pallas_call(
        functools.partial(cross_kernel, seg_total, rows),
        grid_spec=pltpu.PrefetchScalarGridSpec(
            num_scalar_prefetch=1,
            grid=(bins // tile,),
            in_specs=[part_of(lambda partners: REACH)]
            + [other(pair) for pair in range(PAIR_DEV)],
            out_specs=pl.BlockSpec(
                (2, tile, PAIR_DEV, rows, channels), lambda i, partners: (0, i, 0, 0, 0)
            ),
        ),
        out_shape=jax.ShapeDtypeStruct((2, bins, PAIR_DEV, rows, channels), jnp.bfloat16),
    )(partners, *([around] * (1 + PAIR_DEV)))


def per_device(traces, partners):
    channels, seg_local, seg_len = traces.shape
    segs = lax.axis_size("seg")
    blocks = lax.axis_size("offset")
    seg_total = seg_local * segs
    rows = channels // segs
    forward, inverse = make_tables(seg_total, seg_len)
    chunk = spectra_of(traces, jnp.asarray(forward))
    around = gathered(chunk, blocks, segs)
    around = around.reshape(2 * REACH + 1, segs, 2, BINS, seg_local, channels)
    cross = cross_of(partners, around, rows, seg_total)
    cross = cross.reshape(2 * BINS, PAIR_DEV, rows, channels)
    result = jnp.einsum(
        "epij,el->pijl", cross, jnp.asarray(inverse), preferred_element_type=jnp.float32
    )
    return result.astype(jnp.bfloat16)


def solution(mesh):
    in_specs = (P("offset", "seg", None), P("offset", None))
    out_specs = P("offset", "seg", None, None)
    return jax.shard_map(
        per_device, mesh=mesh, in_specs=in_specs, out_specs=out_specs, check_vma=False
    )
```

time: 64.5 us -> 52.8 us (0.82)
  local copies, waits for them, and re-layouts: 6.88 us -> 2.19 us
  Pallas kernels: 51.3 us -> 46.8 us
  other arithmetic: 1.87 us -> 0 us
    pallas_call x1, Pallas kernels: 34.5 us -> 31.1 us  [gathered(): pl.pallas_call(functools.partial(gather_kernel, blocks, segs), out_shape=...]
    convert_element_type x1 -> x0, local copies, waits for them, and re-layouts: 2.38 us -> none  [per_device(): cross = cross_of(places, left.astype(jnp.bfloat16), around, rows, seg_total)]
    slice x2 -> x0, local copies, waits for them, and re-layouts: 1.32 us -> none  [the longest x1 1.3 us: per_device(): around[REACH]]
    sub x1 -> x0, other arithmetic: 1.14 us -> none  [per_device(): places = partners[0] + REACH - lax.axis_index('offset')]
    pallas_call x2, Pallas kernels: 16.8 us -> 15.7 us  [the longest x1 8.56 us: spectra_of(): pl.pallas_call(functools.partial(spectra_kernel, seg_local), grid=(seg_le...]
where the time goes in v2:
time: 52.8 us; the launch traced here: 52.4 us
  Pallas kernels  46.8 us (89%)
  matrix products  3.37 us (6%)
  local copies, waits for them, and re-layouts  2.19 us (4%)
    pallas_call x1, Pallas kernels, gathered(): pl.pallas_call(functools.partial(gather_kernel, blocks, segs), out_shape=...  31.1 us
    pallas_call x1, Pallas kernels, spectra_of(): pl.pallas_call(functools.partial(spectra_kernel, seg_local), grid=(seg_le...  8.56 us
    pallas_call x1, Pallas kernels, cross_of(): pl.pallas_call(functools.partial(cross_kernel, seg_total, rows), grid_spe...  7.14 us
    dot_general x1, matrix products, per_device(): jnp.einsum('epij,el->pijl', cross, jnp.asarray(inverse), preferred_elemen...  3.37 us
    convert_element_type x1, local copies, waits for them, and re-layouts, per_device(): return result.astype(jnp.bfloat16)  2.19 us

profile of v2, /device:TPU:3, one launch (start us, length us, event | category | flops | bytes accessed | tf_op | source)
XLA Modules:
  0.0 52.4 jit_solution(694233904025395040)
XLA Ops:
  0.0 8.6 %shard_map.46.own_ref = bf16[1024,128]{1,0:T(8,128)(2,1)} custom-call(bf16[1024,4096]{1,0:T(8,128)(2,1)} %bitcast.12, bf16[4096,128]{1,0:T(8,128)(2,1)} %constant.4.clone.table_ref), custom_call_target="tpu_custom_call" | custom-call | tf_op jit(solution)/shard_map/pallas_call | solution.py:64
  8.6 31.1 %shard_map.47 = bf16[7,4,1024,128]{3,2,1,0:T(8,128)(2,1)} custom-call(bf16[1024,128]{1,0:T(8,128)(2,1)} %shard_map.46.own_ref), custom_call_target="tpu_custom_call" | custom-call | tf_op jit(solution)/shard_map/pallas_call | solution.py:261
  39.7 0.0 copy-start
  39.7 7.1 %shard_map.48 = bf16[2,64,3,32,128]{4,3,2,1,0:T(8,128)(2,1)} custom-call(s32[1,3]{1,0:T(1,128)} %partners_ref.1, bf16[7,4,2,64,8,128]{5,4,3,2,1,0:T(8,128)(2,1)} %bitcast.7, bf16[7,4,2,64,8,128]{5,4,3,2,1,0:T(8,128)(2,1)} %bitcast.8, bf16[7,4,2,64,8,128]{5,4,3,2,1,0:T(8,128)(2,1)} %bitcast.9, bf16[7,4,2,64,8,128]{5,4,3,2,1,0:T(8,128)(2,1)} %bitcast.10), custom_call_target="tpu_custom_call" | custom-call | tf_op jit(solution)/shard_map/pallas_call | solution.py:321
  46.8 0.0 copy-done
  46.8 3.4 %fusion.2 = bf16[3,32,128,129]{2,3,1,0:T(8,128)(2,1)S(1)} fusion(bf16[128,129,1,1]{0,1,3,2:T(8,128)(2,1)S(1)} %copy-done, bf16[128,3,32,128]{3,2,1,0:T(8,128)(2,1)} %bitcast.11), kind=kOutput, calls=%fused_computation.2 | convolution fusion | flops 407384064 | bytes 6349056 | tf_op jit(solution)/shard_map/epij,el->pijl/dot_general | solution.py:348
  50.2 2.2 %copy.6 = bf16[3,32,128,129]{2,1,3,0:T(8,128)(2,1)} copy(bf16[3,32,128,129]{2,3,1,0:T(8,128)(2,1)S(1)} %fusion.2) | data formatting | bytes 6340608 | tf_op jit(solution)/shard_map/convert_element_type | solution.py:351
Async XLA Ops:
  39.7 7.2 %copy-start = (bf16[128,129,1,1]{0,1,3,2:T(8,128)(2,1)S(1)}, bf16[128,129,1,1]{0,1,3,2:T(8,128)(2,1)}, u32[]{:S(2)}) copy-start(bf16[128,129,1,1]{0,1,3,2:T(8,128)(2,1)} %constant.7) | copy-start | bytes 99076

commit v3 on v2

--- a/solution.py
+++ b/solution.py
@@ -36,16 +36,11 @@
 
 def spectra_kernel(seg_local, traces_ref, table_ref, out_ref, flat, turned):
     step = pl.program_id(0)
+    rows = traces_ref.shape[0]
     entries = table_ref.shape[1]
-    part = jnp.dot(traces_ref[...], table_ref[...], preferred_element_type=jnp.float32)
-
-    @pl.when(step == 0)
-    def _():
-        flat[...] = part
-
-    @pl.when(step > 0)
-    def _():
-        flat[...] += part
+    flat[pl.ds(pl.multiple_of(step * rows, rows), rows), :] = jnp.dot(
+        traces_ref[...], table_ref[...], preferred_element_type=jnp.float32
+    )
 
     @pl.when(step == pl.num_programs(0) - 1)
     def _():
@@ -63,10 +58,10 @@
     tile = 512
     return pl.pallas_call(
         functools.partial(spectra_kernel, seg_local),
-        grid=(seg_len // tile,),
+        grid=(rows // tile,),
         in_specs=[
-            pl.BlockSpec((rows, tile), lambda i: (0, i)),
-            pl.BlockSpec((tile, entries), lambda i: (i, 0)),
+            pl.BlockSpec((tile, seg_len), lambda i: (i, 0)),
+            pl.BlockSpec((seg_len, entries), lambda i: (0, 0)),
         ],
         out_specs=pl.BlockSpec((entries * seg_local, channels), lambda i: (0, 0)),
         out_shape=jax.ShapeDtypeStruct((entries * seg_local, channels), jnp.bfloat16),

time: 52.8 us -> 50.1 us (0.949)
  Pallas kernels: 46.8 us -> 44.2 us
    pallas_call x1, Pallas kernels: 8.56 us -> 5.96 us  [spectra_of(): pl.pallas_call(functools.partial(spectra_kernel, seg_local), grid=(rows /...]
where the time goes in v3:
time: 50.1 us; the launch traced here: 49.8 us
  Pallas kernels  44.2 us (88%)
  matrix products  3.37 us (7%)
  local copies, waits for them, and re-layouts  2.19 us (4%)
    pallas_call x1, Pallas kernels, gathered(): pl.pallas_call(functools.partial(gather_kernel, blocks, segs), out_shape=...  31.1 us
    pallas_call x1, Pallas kernels, cross_of(): pl.pallas_call(functools.partial(cross_kernel, seg_total, rows), grid_spe...  7.14 us
    pallas_call x1, Pallas kernels, spectra_of(): pl.pallas_call(functools.partial(spectra_kernel, seg_local), grid=(rows /...  5.96 us
    dot_general x1, matrix products, per_device(): jnp.einsum('epij,el->pijl', cross, jnp.asarray(inverse), preferred_elemen...  3.37 us
    convert_element_type x1, local copies, waits for them, and re-layouts, per_device(): return result.astype(jnp.bfloat16)  2.19 us

profile of v3, /device:TPU:3, one launch (start us, length us, event | category | flops | bytes accessed | tf_op | source)
XLA Modules:
  0.0 49.8 jit_solution(8125139910517215094)
XLA Ops:
  0.0 6.0 %shard_map.46.own_ref = bf16[1024,128]{1,0:T(8,128)(2,1)} custom-call(bf16[1024,4096]{1,0:T(8,128)(2,1)} %bitcast.12, bf16[4096,128]{1,0:T(8,128)(2,1)} %constant.4.clone.table_ref), custom_call_target="tpu_custom_call" | custom-call | tf_op jit(solution)/shard_map/pallas_call | solution.py:59
  6.0 31.1 %shard_map.47 = bf16[7,4,1024,128]{3,2,1,0:T(8,128)(2,1)} custom-call(bf16[1024,128]{1,0:T(8,128)(2,1)} %shard_map.46.own_ref), custom_call_target="tpu_custom_call" | custom-call | tf_op jit(solution)/shard_map/pallas_call | solution.py:256
  37.1 0.0 copy-start
  37.1 7.1 %shard_map.48 = bf16[2,64,3,32,128]{4,3,2,1,0:T(8,128)(2,1)} custom-call(s32[1,3]{1,0:T(1,128)} %partners_ref.1, bf16[7,4,2,64,8,128]{5,4,3,2,1,0:T(8,128)(2,1)} %bitcast.7, bf16[7,4,2,64,8,128]{5,4,3,2,1,0:T(8,128)(2,1)} %bitcast.8, bf16[7,4,2,64,8,128]{5,4,3,2,1,0:T(8,128)(2,1)} %bitcast.9, bf16[7,4,2,64,8,128]{5,4,3,2,1,0:T(8,128)(2,1)} %bitcast.10), custom_call_target="tpu_custom_call" | custom-call | tf_op jit(solution)/shard_map/pallas_call | solution.py:316
  44.2 0.0 copy-done
  44.2 3.4 %fusion.2 = bf16[3,32,128,129]{2,3,1,0:T(8,128)(2,1)S(1)} fusion(bf16[128,129,1,1]{0,1,3,2:T(8,128)(2,1)S(1)} %copy-done, bf16[128,3,32,128]{3,2,1,0:T(8,128)(2,1)} %bitcast.11), kind=kOutput, calls=%fused_computation.2 | convolution fusion | flops 407384064 | bytes 6349056 | tf_op jit(solution)/shard_map/epij,el->pijl/dot_general | solution.py:343
  47.6 2.2 %copy.6 = bf16[3,32,128,129]{2,1,3,0:T(8,128)(2,1)} copy(bf16[3,32,128,129]{2,3,1,0:T(8,128)(2,1)S(1)} %fusion.2) | data formatting | bytes 6340608 | tf_op jit(solution)/shard_map/convert_element_type | solution.py:346
Async XLA Ops:
  37.1 7.2 %copy-start = (bf16[128,129,1,1]{0,1,3,2:T(8,128)(2,1)S(1)}, bf16[128,129,1,1]{0,1,3,2:T(8,128)(2,1)}, u32[]{:S(2)}) copy-start(bf16[128,129,1,1]{0,1,3,2:T(8,128)(2,1)} %constant.7) | copy-start | bytes 99076
